TPU v7x, 256 devices: a whole 4x4x8 slice. The times are simulated.
256 devices in a mesh: dom: 64 (over x, z_lo, y, core), band: 4 (over z_hi).
Axes of the slice: x: 4, y: 4, z: 8 (z_hi: 4, z_lo: 2; z = z_hi * 2 + z_lo), core: 2. Of those that a mesh axis runs over, the one named last changes fastest.
Arguments:
- states: float32 [12288, 1536], P('dom', 'band'), may hold values from -6 to 6
- inv_mass: float32 [12288], P('dom'), may hold values from 0.5 to 2
- cell_ham: float32 [320, 343, 343], P('dom'), as said below
- cell_nodes: int32 [320, 343], P('dom'), may hold values from 0 to 287, as said below
- send_up: int32 [3072], P('dom'), may hold values from 0 to 191, as said below
- send_down: int32 [3072], P('dom'), may hold values from 0 to 191, as said below
- owner: int32 [64], replicated, may hold values from 0 to 63, each once
- rotation_store: float32 [1536, 1536], P('dom'), may hold values from -0.15625 to 0.15625
Outputs:
- rotated: float32 [12288, 1536], P('dom', 'band')
Inputs may be any that keep to these rules, and one draw needn't show every extreme that they name: `cell_ham`: each cell's matrix is symmetric. `cell_nodes`: each domain's cells name every one of its extended nodes at least once. `send_up`: the 48 entries of one domain are distinct. `send_down`: the 48 entries of one domain are distinct. `owner`: a permutation.
All inputs are finite; a program needn't handle non-finite values.
Results may differ from a plain program's by a relative error of at most 0.00007.
Values sent between devices are 32-bit elements; how exact they have to be, the bound alone decides.
A program may use at most 64 MiB of HBM per device.

v0:
```python
import jax
import jax.numpy as jnp
from jax import lax
from jax.sharding import PartitionSpec as P

filter_center = 2.5
filter_half = 3.5
spectrum_floor = -4.0
sigma_one = filter_half / (spectrum_floor - filter_center)
sigma_two = 1.0 / (2.0 / sigma_one - sigma_one)


def with_halo(block, sides, width):
    for axis, dim in sides:
        count = lax.axis_size(axis)
        forward = [(i, i + 1) for i in range(count - 1)]
        forward.append((count - 1, 0))
        backward = [(target, source) for source, target in forward]
        low = lax.ppermute(
            lax.slice_in_dim(block, block.shape[dim] - width, None, axis=dim), axis, forward
        )
        high = lax.ppermute(lax.slice_in_dim(block, 0, width, axis=dim), axis, backward)
        block = jnp.concatenate([low, block, high], axis=dim)
    return block


def apply_operator(values, inv_mass, cell_ham, cell_nodes, send_up, send_down):
    owned_count = values.shape[0]
    ghost_count = send_up.shape[0]
    block_cols = values.shape[1]
    scaled = values * inv_mass[:, None]
    outgoing = jnp.concatenate([scaled[send_down], scaled[send_up]], axis=0)
    padded = with_halo(outgoing, (("dom", 0),), ghost_count)
    extended = jnp.concatenate([scaled, padded[:ghost_count], padded[3 * ghost_count :]], axis=0)
    gathered = extended[cell_nodes]
    products = jnp.einsum(
        "cij,cjs->cis",
        cell_ham,
        gathered,
        precision=lax.Precision.HIGHEST,
        preferred_element_type=jnp.float32,
    )
    empty = jnp.zeros((owned_count + 2 * ghost_count, block_cols), jnp.float32)
    assembled = empty.at[cell_nodes.reshape(-1)].add(products.reshape(-1, block_cols))
    returning = assembled[owned_count:]
    returned = with_halo(returning, (("dom", 0),), ghost_count)
    result = assembled[:owned_count].at[send_down].add(returned[:ghost_count])
    result = result.at[send_up].add(returned[3 * ghost_count :])
    return result * inv_mass[:, None]


def shards(states, inv_mass, cell_ham, cell_nodes, send_up, send_down, owner, rotation_store):
    block_cols = states.shape[1]
    panel_rows = rotation_store.shape[0]
    filtered_one = (
        sigma_one
        / filter_half
        * (
            apply_operator(states, inv_mass, cell_ham, cell_nodes, send_up, send_down)
            - filter_center * states
        )
    )
    applied = apply_operator(filtered_one, inv_mass, cell_ham, cell_nodes, send_up, send_down)
    filtered_two = (
        2.0 * sigma_two / filter_half * (applied - filter_center * filtered_one)
        - sigma_one * sigma_two * states
    )
    row_index = (
        owner[:, None] * panel_rows + jnp.arange(panel_rows, dtype=jnp.int32)[None, :]
    ).reshape(-1)
    band_index = lax.axis_index("band")
    all_rows = lax.all_gather(rotation_store, "dom", axis=0, tiled=True)
    block_index = lax.dynamic_slice_in_dim(row_index, band_index * block_cols, block_cols, 0)
    own_rows = all_rows[block_index]
    partial_term = jnp.dot(
        filtered_two, own_rows, precision=lax.Precision.HIGHEST, preferred_element_type=jnp.float32
    )
    rotated = lax.psum_scatter(partial_term, "band", scatter_dimension=1, tiled=True)
    return rotated


def solution(mesh):
    in_specs = (
        P("dom", "band"),
        P("dom"),
        P("dom", None, None),
        P("dom", None),
        P("dom"),
        P("dom"),
        P(),
        P("dom", None),
    )
    out_specs = P("dom", "band")
    return jax.shard_map(shards, mesh=mesh, in_specs=in_specs, out_specs=out_specs, check_vma=False)
```

profile of v0, /device:TPU:1, one launch (start us, length us, event | category | flops | bytes accessed | tf_op | source)
XLA Modules:
  0.0 192.5 jit_solution(3968801217329243679)
XLA Ops:
  6.5 0.7 all-gather.2.cloned.1.call-update
  7.3 0.7 compare_select_fusion.3
  8.0 0.6 copy-done.9
  8.6 1.1 broadcast_multiply_fusion
  9.6 0.6 gather_fusion.1
  10.3 3.3 %collective-permute-start.1 = (f32[48,384]{1,0:T(8,128)S(1)}, f32[48,384]{1,0:T(8,128)S(1)}, u32[]{:S(2)}, u32[]{:S(2)}) collective-permute-start(f32[48,384]{1,0:T(8,128)S(1)} %gather_fusion.1), channel_id=1, source_target_pairs={{4,0},{8,4},{12,8},{16,12},{20,16},{24,20},{28,24},{32,28},{36,32}... | collective-permute-start | bytes 221192 | tf_op jit(solution)/shard_map/ppermute | solution.py:22
  13.6 0.7 compare_select_fusion.4
  14.3 0.6 gather_fusion
  14.9 0.1 collective-permute-start
  15.0 0.8 reshape.45
  15.8 0.7 compare_select_fusion.1
  16.5 0.1 reshape.66
  16.6 0.7 broadcast_multiply_fusion.2
  17.3 0.7 iota_add_fusion
  18.0 2.2 %collective-permute-done = f32[48,384]{1,0:T(8,128)} collective-permute-done((f32[48,384]{1,0:T(8,128)S(1)}, f32[48,384]{1,0:T(8,128)}, u32[]{:S(2)}, u32[]{:S(2)}) %collective-permute-start) | collective-permute-done | bytes 73760 | tf_op jit(solution)/shard_map/ppermute | solution.py:19
  20.1 0.9 pad_maximum_fusion
  21.1 5.5 %gather_fusion.2 = f32[1715,384]{1,0:T(8,128)} fusion(f32[288,384]{1,0:T(8,128)S(1)} %pad_maximum_fusion, s32[2048]{0:T(1024)S(1)} %pad_clamp_fusion), kind=kCustom, calls=%fused_computation.2 | custom fusion | bytes 5275340 | tf_op jit(solution)/shard_map/gather | solution.py:35
  26.5 3.5 %reshape.65 = f32[5,343,384]{2,1,0:T(8,128)} reshape(f32[1715,384]{1,0:T(8,128)} %gather_fusion.2) | data formatting | bytes 5268480 | tf_op jit(solution)/shard_map/gather | solution.py:35
  30.1 9.0 %convolution_bitcast_fusion.1 = f32[5,343,384]{2,1,0:T(8,128)} fusion(f32[5,343,384]{2,1,0:T(8,128)} %reshape.65, f32[5,343,343]{2,1,0:T(8,128)S(1)} %copy-done), kind=kOutput, calls=%fused_computation.14 | convolution fusion | flops 2710632960 | bytes 7621460 | tf_op jit(solution)/shard_map/cij,cjs->cis/dot_general | solution.py:36
  39.1 3.6 %reshape.108 = f32[1715,384]{1,0:T(8,128)} reshape(f32[5,343,384]{2,1,0:T(8,128)} %convolution_bitcast_fusion.1) | data formatting | bytes 5268480 | tf_op jit(solution)/shard_map/reshape | solution.py:44
  42.7 13.3 %scatter_custom_fusion = f32[288,384]{1,0:T(8,128)S(1)} fusion(s32[1715]{0:T(1024)S(1)} %fusion.17, f32[1715,384]{1,0:T(8,128)} %reshape.108, f32[]{:T(128)} %constant.13.clone.1), kind=kCustom, calls=%fused_computation.28 | custom fusion | flops 658560 | bytes 442880 | tf_op jit(solution)/shard_map/scatter-add | solution.py:44
  56.0 0.7 fusion.23
  56.7 7.2 %collective-permute-start.3 = (f32[48,384]{1,0:T(8,128)}, f32[48,384]{1,0:T(8,128)S(1)}, u32[]{:S(2)}, u32[]{:S(2)}) collective-permute-start(f32[48,384]{1,0:T(8,128)} %get-tuple-element.7), channel_id=1, source_target_pairs={{4,0},{8,4},{12,8},{16,12},{20,16},{24,20},{28,24},{32,28},{36,32}... | collective-permute-start | bytes 221192 | tf_op jit(solution)/shard_map/ppermute | solution.py:22
  63.9 0.6 broadcast_multiply_fusion.1
  64.5 0.1 add.74
  64.6 1.0 slice.44
  65.6 1.6 scatter_fusion
  67.1 1.0 scatter_fusion.1
  68.2 0.8 fusion.7
  69.0 0.6 gather_fusion.4
  69.6 0.6 gather_fusion.3
  70.3 6.7 %collective-permute-start.5 = (f32[48,384]{1,0:T(8,128)S(1)}, f32[48,384]{1,0:T(8,128)S(1)}, u32[]{:S(2)}, u32[]{:S(2)}) collective-permute-start(f32[48,384]{1,0:T(8,128)S(1)} %gather_fusion.4), channel_id=1, source_target_pairs={{4,0},{8,4},{12,8},{16,12},{20,16},{24,20},{28,24},{32,28},{36,32}... | collective-permute-start | bytes 221192 | tf_op jit(solution)/shard_map/ppermute | solution.py:22
  77.0 0.8 collective-permute-done.5
  77.9 4.7 %collective-permute-done.4 = f32[48,384]{1,0:T(8,128)S(1)} collective-permute-done((f32[48,384]{1,0:T(8,128)S(1)}, f32[48,384]{1,0:T(8,128)S(1)}, u32[]{:S(2)}, u32[]{:S(2)}) %collective-permute-start.4) | collective-permute-done | bytes 73760 | tf_op jit(solution)/shard_map/ppermute | solution.py:19
  82.6 1.0 pad_maximum_fusion.1
  83.6 5.5 %gather_fusion.5 = f32[1715,384]{1,0:T(8,128)} fusion(f32[288,384]{1,0:T(8,128)S(1)} %pad_maximum_fusion.1, s32[2048]{0:T(1024)S(1)} %pad_clamp_fusion), kind=kCustom, calls=%fused_computation.5 | custom fusion | bytes 5275340 | tf_op jit(solution)/shard_map/gather | solution.py:35
  89.0 3.6 %reshape.89 = f32[5,343,384]{2,1,0:T(8,128)} reshape(f32[1715,384]{1,0:T(8,128)} %gather_fusion.5) | data formatting | bytes 5268480 | tf_op jit(solution)/shard_map/gather | solution.py:35
  92.6 9.0 %convolution_bitcast_fusion = f32[5,343,384]{2,1,0:T(8,128)} fusion(f32[5,343,384]{2,1,0:T(8,128)} %reshape.89, f32[5,343,343]{2,1,0:T(8,128)S(1)} %copy-done), kind=kOutput, calls=%fused_computation.13 | convolution fusion | flops 2710632960 | bytes 7621460 | tf_op jit(solution)/shard_map/cij,cjs->cis/dot_general | solution.py:36
  101.6 3.6 %reshape.132 = f32[1715,384]{1,0:T(8,128)} reshape(f32[5,343,384]{2,1,0:T(8,128)} %convolution_bitcast_fusion) | data formatting | bytes 5268480 | tf_op jit(solution)/shard_map/reshape | solution.py:44
  105.2 13.2 %scatter_custom_fusion.3 = f32[288,384]{1,0:T(8,128)S(1)} fusion(s32[1715]{0:T(1024)} %copy-done.8, f32[1715,384]{1,0:T(8,128)} %reshape.132, f32[]{:T(128)} %constant.13.clone.1), kind=kCustom, calls=%fused_computation.26 | custom fusion | flops 658560 | bytes 442880 | tf_op jit(solution)/shard_map/scatter-add | solution.py:44
  118.4 0.7 fusion.22
  119.1 7.2 %collective-permute-start.7 = (f32[48,384]{1,0:T(8,128)}, f32[48,384]{1,0:T(8,128)S(1)}, u32[]{:S(2)}, u32[]{:S(2)}) collective-permute-start(f32[48,384]{1,0:T(8,128)} %get-tuple-element.5), channel_id=1, source_target_pairs={{4,0},{8,4},{12,8},{16,12},{20,16},{24,20},{28,24},{32,28},{36,32}... | collective-permute-start | bytes 221192 | tf_op jit(solution)/shard_map/ppermute | solution.py:22
  126.4 1.0 slice.47
  127.4 1.0 scatter_fusion.2
  128.4 1.2 scatter_fusion.3
  129.7 8.0 %gather_fusion.6 = f32[384,1536]{1,0:T(8,128)} fusion(f32[1536,1536]{1,0:T(8,128)} %all-gather.2.cloned.1.call-done, s32[1024]{0:T(1024)S(1)} %pad_clamp_fusion.1), kind=kCustom, calls=%fused_computation.6 | custom fusion | bytes 4720128 | tf_op jit(solution)/shard_map/gather | solution.py:74
  137.7 4.9 %fusion = f32[192,1536]{1,0:T(8,128)} fusion(f32[384,1536]{1,0:T(8,128)} %gather_fusion.6, f32[192,384]{1,0:T(8,128)S(1)} %copy-done.3, f32[192,384]{1,0:T(8,128)S(1)} %scatter_fusion.3, f32[192,384]{1,0:T(8,128)S(1)} %scatter_fusion.1, f32[192]{0:T(256)S(1)} %copy-done.7), kind=kOutput, calls=%fused_computation.17 | convolution fusion | flops 1359618048 | bytes 4424448 | tf_op jit(solution)/shard_map/dot_general | solution.py:75
  142.6 43.0 %reduce-scatter.2.cloned.1.call-done = f32[192,384]{1,0:T(8,128)} async-done(((f32[192,1536]{1,0:T(8,128)}), f32[192,384]{1,0:T(8,128)}) %reduce-scatter.2.cloned.1.call-update) | async-done | bytes 294928 | tf_op jit(solution)/shard_map/reduce_scatter | solution.py:78
  (47 shorter events, 0.3 us)
Async XLA Ops:
  6.5 23.5 %copy-start = (f32[5,343,343]{2,1,0:T(8,128)S(1)}, f32[5,343,343]{2,1,0:T(8,128)}, u32[]{:S(2)}) copy-start(f32[5,343,343]{2,1,0:T(8,128)} %param.10) | copy-start | bytes 7058944
  6.5 123.2 %all-gather.2.cloned.1.call-start = ((), (), s32[]{:S(2)}) async-start(), calls=%async_computation.1 | async-start | bytes 9584640 | tf_op jit(solution)/shard_map/all_gather | solution.py:72
  7.3 178.4 %reduce-scatter.2.cloned.1.call-start = ((), (), s32[]{:S(2)}) async-start(), calls=%async_computation.2 | async-start | bytes 1474560 | tf_op jit(solution)/shard_map/reduce_scatter | solution.py:78
  8.0 0.6 copy-start.9
  10.3 7.7 %collective-permute-start.1 = (f32[48,384]{1,0:T(8,128)S(1)}, f32[48,384]{1,0:T(8,128)S(1)}, u32[]{:S(2)}, u32[]{:S(2)}) collective-permute-start(f32[48,384]{1,0:T(8,128)S(1)} %gather_fusion.1), channel_id=1, source_target_pairs={{4,0},{8,4},{12,8},{16,12},{20,16},{24,20},{28,24},{32,28},{36,32}... | collective-permute-start | bytes 221192 | tf_op jit(solution)/shard_map/ppermute | solution.py:22
  14.3 3.0 %copy-start.12 = (s32[48]{0:T(128)}, s32[48]{0:T(128)S(1)}, u32[]{:S(2)}) copy-start(s32[48]{0:T(128)S(1)} %compare_select_fusion.4) | copy-start | bytes 580
  14.9 5.2 %collective-permute-start = (f32[48,384]{1,0:T(8,128)S(1)}, f32[48,384]{1,0:T(8,128)}, u32[]{:S(2)}, u32[]{:S(2)}) collective-permute-start(f32[48,384]{1,0:T(8,128)S(1)} %gather_fusion), channel_id=1, source_target_pairs={{0,4},{4,8},{8,12},{12,16},{16,20},{20,24},{24,28},{28,32},{32,36}... | collective-permute-start | bytes 221192 | tf_op jit(solution)/shard_map/ppermute | solution.py:19
  16.6 26.1 %copy-start.8 = (s32[1715]{0:T(1024)}, s32[1715]{0:T(1024)S(1)}, u32[]{:S(2)}) copy-start(s32[1715]{0:T(1024)S(1)} %fusion.17) | copy-start | bytes 20584
  39.1 24.8 %copy-start.7 = (f32[192]{0:T(256)S(1)}, f32[192]{0:T(256)}, u32[]{:S(2)}) copy-start(f32[192]{0:T(256)} %param.9) | copy-start | bytes 2308
  39.1 25.4 %copy-start.6 = (s32[64,24]{1,0:T(8,128)S(1)}, s32[64,24]{1,0:T(8,128)}, u32[]{:S(2)}) copy-start(s32[64,24]{1,0:T(8,128)} %iota_add_fusion) | copy-start | bytes 18436
  39.1 26.5 %copy-start.10 = (s32[48]{0:T(128)S(1)}, s32[48]{0:T(128)}, u32[]{:S(2)}) copy-start(s32[48]{0:T(128)} %copy-done.9) | copy-start | bytes 580
  42.7 24.5 %copy-start.13 = (s32[48]{0:T(128)S(1)}, s32[48]{0:T(128)}, u32[]{:S(2)}) copy-start(s32[48]{0:T(128)} %copy-done.12) | copy-start | bytes 580
  42.7 25.5 %copy-start.2 = (f32[192,384]{1,0:T(8,128)S(1)}, f32[192,384]{1,0:T(8,128)}, u32[]{:S(2)}) copy-start(f32[192,384]{1,0:T(8,128)} %param.8) | copy-start | bytes 884740
  56.0 8.6 %copy-start.4 = (f32[288,384]{1,0:T(8,128)}, f32[288,384]{1,0:T(8,128)S(1)}, u32[]{:S(2)}) copy-start(f32[288,384]{1,0:T(8,128)S(1)} %scatter_custom_fusion) | copy-start | bytes 1327108
  56.7 8.9 %collective-permute-start.2 = (f32[48,384]{1,0:T(8,128)}, f32[48,384]{1,0:T(8,128)}, u32[]{:S(2)}, u32[]{:S(2)}) collective-permute-start(f32[48,384]{1,0:T(8,128)} %get-tuple-element.8), channel_id=1, source_target_pairs={{0,4},{4,8},{8,12},{12,16},{16,20},{20,24},{24,28},{28,32},{32,36}... | collective-permute-start | bytes 221192 | tf_op jit(solution)/shard_map/ppermute | solution.py:19
  56.7 10.4 %collective-permute-start.3 = (f32[48,384]{1,0:T(8,128)}, f32[48,384]{1,0:T(8,128)S(1)}, u32[]{:S(2)}, u32[]{:S(2)}) collective-permute-start(f32[48,384]{1,0:T(8,128)} %get-tuple-element.7), channel_id=1, source_target_pairs={{4,0},{8,4},{12,8},{16,12},{20,16},{24,20},{28,24},{32,28},{36,32}... | collective-permute-start | bytes 221192 | tf_op jit(solution)/shard_map/ppermute | solution.py:22
  69.0 8.9 %copy-start.1 = (f32[192,384]{1,0:T(8,128)}, f32[192,384]{1,0:T(8,128)S(1)}, u32[]{:S(2)}) copy-start(f32[192,384]{1,0:T(8,128)S(1)} %fusion.7) | copy-start | bytes 884740
  70.3 7.6 %collective-permute-start.5 = (f32[48,384]{1,0:T(8,128)S(1)}, f32[48,384]{1,0:T(8,128)S(1)}, u32[]{:S(2)}, u32[]{:S(2)}) collective-permute-start(f32[48,384]{1,0:T(8,128)S(1)} %gather_fusion.4), channel_id=1, source_target_pairs={{4,0},{8,4},{12,8},{16,12},{20,16},{24,20},{28,24},{32,28},{36,32}... | collective-permute-start | bytes 221192 | tf_op jit(solution)/shard_map/ppermute | solution.py:22
  76.9 5.6 %collective-permute-start.4 = (f32[48,384]{1,0:T(8,128)S(1)}, f32[48,384]{1,0:T(8,128)S(1)}, u32[]{:S(2)}, u32[]{:S(2)}) collective-permute-start(f32[48,384]{1,0:T(8,128)S(1)} %gather_fusion.3), channel_id=1, source_target_pairs={{0,4},{4,8},{8,12},{12,16},{16,20},{20,24},{24,28},{28,32},{32,36}... | collective-permute-start | bytes 221192 | tf_op jit(solution)/shard_map/ppermute | solution.py:19
  101.6 25.8 %copy-start.11 = (s32[48]{0:T(128)S(1)}, s32[48]{0:T(128)}, u32[]{:S(2)}) copy-start(s32[48]{0:T(128)} %copy-done.9) | copy-start | bytes 580
  101.6 26.8 %copy-start.14 = (s32[48]{0:T(128)S(1)}, s32[48]{0:T(128)}, u32[]{:S(2)}) copy-start(s32[48]{0:T(128)} %copy-done.12) | copy-start | bytes 580
  118.4 7.9 %copy-start.5 = (f32[288,384]{1,0:T(8,128)}, f32[288,384]{1,0:T(8,128)S(1)}, u32[]{:S(2)}) copy-start(f32[288,384]{1,0:T(8,128)S(1)} %scatter_custom_fusion.3) | copy-start | bytes 1327108
  119.1 8.2 %collective-permute-start.6 = (f32[48,384]{1,0:T(8,128)S(1)}, f32[48,384]{1,0:T(8,128)S(1)}, u32[]{:S(2)}, u32[]{:S(2)}) collective-permute-start(f32[48,384]{1,0:T(8,128)S(1)} %get-tuple-element.6), channel_id=1, source_target_pairs={{0,4},{4,8},{8,12},{12,16},{16,20},{20,24},{24,28},{28,32},{32,36}... | collective-permute-start | bytes 221192 | tf_op jit(solution)/shard_map/ppermute | solution.py:19
  119.1 9.3 %collective-permute-start.7 = (f32[48,384]{1,0:T(8,128)}, f32[48,384]{1,0:T(8,128)S(1)}, u32[]{:S(2)}, u32[]{:S(2)}) collective-permute-start(f32[48,384]{1,0:T(8,128)} %get-tuple-element.5), channel_id=1, source_target_pairs={{4,0},{8,4},{12,8},{16,12},{20,16},{24,20},{28,24},{32,28},{36,32}... | collective-permute-start | bytes 221192 | tf_op jit(solution)/shard_map/ppermute | solution.py:22
  129.7 8.1 %copy-start.3 = (f32[192,384]{1,0:T(8,128)S(1)}, f32[192,384]{1,0:T(8,128)}, u32[]{:S(2)}) copy-start(f32[192,384]{1,0:T(8,128)} %param.8) | copy-start | bytes 884740
Sparse Core Ops, SparseCore 0:
  9.2 120.3 all-gather.1
  142.8 42.8 reduce-scatter.1
where the time goes:
time: 193 us; the launch traced here: 192 us
  waiting for transfers between devices  51.5 us (27%)
  local copies, waits for them, and re-layouts  40.7 us (21%)
  other arithmetic  39.2 us (20%)
  starting transfers between devices  24.5 us (13%)
  matrix products  22.9 us (12%)
  between operations  13.7 us (7%)
    reduce_scatter x1, waiting for transfers between devices, shards(): lax.psum_scatter(partial_term, 'band', scatter_dimension=1, tiled=True)  43 us
    scatter-add x2, other arithmetic, apply_operator(): empty.at[cell_nodes.reshape(-1)].add(products.reshape(-1, block_cols))  26.5 us
    ppermute x4, starting transfers between devices, with_halo(): lax.ppermute(lax.slice_in_dim(block, 0, width, axis=dim), axis, backward)  24.4 us
    gather x4, local copies, waits for them, and re-layouts, apply_operator(): gathered = extended[cell_nodes]  18 us
    dot_general x2, matrix products, apply_operator(): jnp.einsum('cij,cjs->cis', cell_ham, gathered, precision=lax.Precision.HI...  18 us
    gather x1, local copies, waits for them, and re-layouts, shards(): own_rows = all_rows[block_index]  8.03 us
    reshape x2, local copies, waits for them, and re-layouts, apply_operator(): products.reshape(-1, block_cols)  7.17 us
    ppermute x4, waiting for transfers between devices, with_halo(): lax.ppermute(lax.slice_in_dim(block, block.shape[dim] - width, None, axis...  6.89 us
  transfers between devices with their start and end apart: 10, of which 4 were waited for; matrix products, arithmetic and copies ran while one was open for 46% of the time, Pallas kernels for 0%

commit v1 on v0

v1 whole, which is shorter than its diff:
```python
import math

import jax
import jax.numpy as jnp
from jax import lax
from jax.experimental import pallas as pl
from jax.experimental.pallas import tpu as pltpu
from jax.sharding import PartitionSpec as P

filter_center = 2.5
filter_half = 3.5
spectrum_floor = -4.0
sigma_one = filter_half / (spectrum_floor - filter_center)
sigma_two = 1.0 / (2.0 / sigma_one - sigma_one)
scale = 2.0 * sigma_one * sigma_two / filter_half**2
root_a = filter_center + filter_half / math.sqrt(2.0)
root_b = filter_center - filter_half / math.sqrt(2.0)

OWN = 192
GHOST = 48
COLS = 384
CELLS = 5
CN = 343
EXT = 320
FIRST = 128
PANEL = 24
STATES = 1536
HALF = OWN // 2

f32 = jnp.float32
bf16 = jnp.bfloat16


def split(x):
    high = x.astype(bf16)
    low = (x - high.astype(f32)).astype(bf16)
    return high, low


def dot(a, b):
    return jnp.dot(a, b, preferred_element_type=f32)


def mm2(pick, x):
    high, low = split(x)
    return dot(pick, high) + dot(pick, low)


def mm3(ah, al, bh, bl):
    return dot(ah, bh) + (dot(al, bh) + dot(ah, bl))


def column(row, count):
    wide = jnp.broadcast_to(row, (count, count))
    same = lax.broadcasted_iota(jnp.int32, (count, count), 0) == lax.broadcasted_iota(
        jnp.int32, (count, count), 1
    )
    return jnp.sum(jnp.where(same, wide, 0.0), axis=1, keepdims=True)


def one_hot(condition):
    return jnp.where(condition, 1.0, 0.0).astype(bf16)


def kernel(
    states, mass, ham, nodes, sup, sdn, owner, rot, out,
    xv, mv, hv, nv, upv, dnv, ownv, rb,
    gs, gr, rs, rr, amat, ah, al, fg, rh, rl, ov,
    ld, rsend, first_sem, second_sem, far_sem, mate_sem,
    gsend, grecv, bsend, brecv,
):
    d = lax.axis_index("dom")
    band = lax.axis_index("band")
    core = lax.rem(d, 2)
    y = lax.rem(d // 2, 4)
    zl = lax.rem(d // 8, 2)
    x = d // 16

    def dom_of(x_, y_, zl_, core_):
        return ((x_ * 2 + zl_) * 4 + y_) * 2 + core_

    def along_first(k):
        return dom_of(lax.rem(x + k * (1 - core), 4), lax.rem(y + k * core, 4), zl, core)

    def along_second(k):
        return dom_of(lax.rem(x + k * core, 4), lax.rem(y + k * (1 - core), 4), zl, core)

    f0 = x * (1 - core) + y * core
    s0 = y * (1 - core) + x * core

    def slot(s, f, z):
        return ((core * 4 + s) * 4 + f) * 2 + z

    up = (lax.rem(d + 1, 64), band)
    down = (lax.rem(d + 63, 64), band)
    f_up, f_down = (along_first(1), band), (along_first(3), band)
    s_up, s_down = (along_second(1), band), (along_second(3), band)
    z_mate = (dom_of(x, y, 1 - zl, core), band)
    mate = (dom_of(x, y, zl, 1 - core), band)
    b_up, b_down = (d, lax.rem(band + 1, 4)), (d, lax.rem(band + 3, 4))

    barrier = pltpu.get_barrier_semaphore()
    peers = (up, down, f_up, f_down, s_up, s_down, z_mate, mate, b_up, b_down)
    for peer in peers:
        pl.semaphore_signal(barrier, inc=1, device_id=peer, device_id_type=pl.DeviceIdType.MESH)

    def send(src, dst, ssem, rsem, peer):
        copy = pltpu.make_async_remote_copy(
            src_ref=src, dst_ref=dst, send_sem=ssem, recv_sem=rsem,
            device_id=peer, device_id_type=pl.DeviceIdType.MESH,
        )
        copy.start()
        return copy

    def arrived(dst, rsem):
        pltpu.make_async_copy(dst, dst, rsem).wait()

    my_columns = rot.at[:, pl.ds(pl.multiple_of(band * COLS, 128), COLS)]
    loads = [
        pltpu.make_async_copy(states, xv, ld.at[0]),
        pltpu.make_async_copy(mass, mv, ld.at[1]),
        pltpu.make_async_copy(sup, upv, ld.at[2]),
        pltpu.make_async_copy(sdn, dnv, ld.at[3]),
        pltpu.make_async_copy(nodes, nv, ld.at[4]),
        pltpu.make_async_copy(ham, hv, ld.at[5]),
        pltpu.make_async_copy(my_columns, rb.at[slot(s0, f0, zl)], ld.at[6]),
        pltpu.make_async_copy(owner, ownv, ld.at[7]),
    ]
    for load in loads:
        load.start()

    for load in loads[:4]:
        load.wait()
    up_row, down_row = upv[...], dnv[...]
    m = column(mv[...], OWN)
    lanes = lax.broadcasted_iota(jnp.int32, (GHOST, OWN), 1)
    pick_up = one_hot(column(up_row.astype(f32), GHOST).astype(jnp.int32) == lanes)
    pick_down = one_hot(column(down_row.astype(f32), GHOST).astype(jnp.int32) == lanes)
    rows = lax.broadcasted_iota(jnp.int32, (OWN, GHOST), 0)
    add_up = one_hot(rows == up_row)
    add_down = one_hot(rows == down_row)
    states_scaled = xv[...] * m

    def ghosts_out(k, values):
        high, low = split(values)
        gs[k, pl.ds(0, GHOST)] = dot(pick_up, high) + dot(pick_up, low)
        gs[k, pl.ds(GHOST, GHOST)] = dot(pick_down, high) + dot(pick_down, low)
        return [
            send(gs.at[k, pl.ds(0, GHOST)], gr.at[k, pl.ds(0, GHOST)],
                 gsend.at[k, 0], grecv.at[k, 0], up),
            send(gs.at[k, pl.ds(GHOST, GHOST)], gr.at[k, pl.ds(GHOST, GHOST)],
                 gsend.at[k, 1], grecv.at[k, 1], down),
        ]

    def apply_own(values):
        high, low = split(values)
        return mm3(ah[:, FIRST:], al[:, FIRST:], high, low)

    def ghosts_in(k):
        for side in range(2):
            part = gr.at[k, pl.ds(side * GHOST, GHOST)]
            arrived(part, grecv.at[k, side])
        high, low = split(gr[k])
        return mm3(ah[:, : 2 * GHOST], al[:, : 2 * GHOST], high, low)

    def sums_out(k, total):
        rs[k] = total[: 2 * GHOST]
        return [
            send(rs.at[k, pl.ds(0, GHOST)], rr.at[k, pl.ds(0, GHOST)],
                 gsend.at[k, 2], grecv.at[k, 2], down),
            send(rs.at[k, pl.ds(GHOST, GHOST)], rr.at[k, pl.ds(GHOST, GHOST)],
                 gsend.at[k, 3], grecv.at[k, 3], up),
        ]

    def sums_in(k):
        for side in range(2):
            arrived(rr.at[k, pl.ds(side * GHOST, GHOST)], grecv.at[k, 2 + side])
        return mm2(add_up, rr[k, pl.ds(0, GHOST)]) + mm2(add_down, rr[k, pl.ds(GHOST, GHOST)])

    pl.semaphore_wait(barrier, len(peers))

    sends = []
    sends += ghosts_out(0, states_scaled)

    sem = iter(range(64))

    def panel(src, s, f, z, rsem, peer):
        sends.append(send(src, rb.at[slot(s, f, z)], rsend.at[next(sem)], rsem, peer))

    def pair(s, f, rsem, peer):
        both = rb.at[pl.ds(slot(s, f, 0), 2)]
        sends.append(send(both, both, rsend.at[next(sem)], rsem, peer))

    def block(s):
        all_of = rb.at[pl.ds(slot(s, 0, 0), 8)]
        sends.append(send(all_of, all_of, rsend.at[next(sem)], mate_sem.at[s], mate))

    panel(my_columns, s0, f0, zl, first_sem.at[f0, zl], z_mate)
    panel(my_columns, s0, f0, zl, first_sem.at[f0, zl], f_up)
    panel(my_columns, s0, f0, zl, first_sem.at[f0, zl], f_down)

    f_next, f_last, f_far = lax.rem(f0 + 1, 4), lax.rem(f0 + 3, 4), lax.rem(f0 + 2, 4)
    s_next, s_last, s_far = lax.rem(s0 + 1, 4), lax.rem(s0 + 3, 4), lax.rem(s0 + 2, 4)

    def one_cell(c):
        node = nv[pl.ds(c, 1)]
        where = jnp.where(node < OWN, node + FIRST, node - OWN)
        place = one_hot(lax.broadcasted_iota(jnp.int32, (EXT, CN), 0) == where)
        high, low = split(hv[c])
        nt = (((1,), (1,)), ((), ()))
        half = lax.dot_general(high, place, nt, preferred_element_type=f32)
        half = half + lax.dot_general(low, place, nt, preferred_element_type=f32)
        total = mm2(place, half)
        if c == 0:
            amat[...] = total
        else:
            amat[...] += total

    loads[4].wait()
    loads[5].wait()
    one_cell(0)
    loads[6].wait()

    one_cell(1)
    other = 1 - zl
    arrived(rb.at[slot(s0, f0, other)], first_sem.at[f0, other])
    panel(rb.at[slot(s0, f0, other)], s0, f0, other, first_sem.at[f0, other], f_up)
    panel(rb.at[slot(s0, f0, other)], s0, f0, other, first_sem.at[f0, other], f_down)
    pair(s0, f0, second_sem.at[s0, f0], s_up)
    pair(s0, f0, second_sem.at[s0, f0], s_down)
    one_cell(2)
    one_cell(3)

    arrived(rb.at[slot(s0, f_last, 0)], first_sem.at[f_last, 0])
    panel(rb.at[slot(s0, f_last, 0)], s0, f_last, 0, first_sem.at[f_last, 0], f_up)
    arrived(rb.at[slot(s0, f_next, 1)], first_sem.at[f_next, 1])
    panel(rb.at[slot(s0, f_next, 1)], s0, f_next, 1, first_sem.at[f_next, 1], f_down)
    arrived(rb.at[slot(s0, f_last, 1)], first_sem.at[f_last, 1])
    pair(s0, f_last, second_sem.at[s0, f_last], s_up)
    pair(s0, f_last, second_sem.at[s0, f_last], s_down)
    arrived(rb.at[slot(s0, f_next, 0)], first_sem.at[f_next, 0])
    pair(s0, f_next, second_sem.at[s0, f_next], s_up)
    pair(s0, f_next, second_sem.at[s0, f_next], s_down)

    one_cell(4)
    ahv, alv = split(amat[...])
    ah[...] = ahv
    al[...] = alv
    total = apply_own(states_scaled)
    total = total + ghosts_in(0)
    sends += sums_out(0, total)

    def relay(f):
        arrived(rb.at[pl.ds(slot(s_last, f, 0), 2)], second_sem.at[s_last, f])
        panel(rb.at[slot(s_last, f, 0)], s_last, f, 0, far_sem.at[f, 0], s_up)
        arrived(rb.at[pl.ds(slot(s_next, f, 0), 2)], second_sem.at[s_next, f])
        panel(rb.at[slot(s_next, f, 1)], s_next, f, 1, far_sem.at[f, 1], s_down)

    for z in range(2):
        arrived(rb.at[slot(s0, f_far, z)], first_sem.at[f_far, z])
    pair(s0, f_far, second_sem.at[s0, f_far], s_up)
    pair(s0, f_far, second_sem.at[s0, f_far], s_down)
    block(s0)
    relay(f0)
    relay(f_last)
    relay(f_next)

    step = m * (total[FIRST:] + sums_in(0)) - root_a * xv[...]
    step_scaled = step * m
    sends += ghosts_out(1, step_scaled)
    relay(f_far)
    block(s_last)
    block(s_next)
    total = apply_own(step_scaled)
    total = total + ghosts_in(1)
    sends += sums_out(1, total)
    for f in (f0, f_last, f_next, f_far):
        for z in range(2):
            arrived(rb.at[slot(s_far, f, z)], far_sem.at[f, z])
    block(s_far)

    mate_s0 = s0 * 0 + f0
    for k in (0, 3, 1, 2):
        s = lax.rem(mate_s0 + k, 4)
        theirs = rb.at[pl.ds((((1 - core) * 4 + s) * 4) * 2, 8)]
        arrived(theirs, mate_sem.at[s])
    loads[7].wait()

    def place_of(p):
        o = ownv[p]
        c_, y_, z_, x_ = lax.rem(o, 2), lax.rem(o // 2, 4), lax.rem(o // 8, 2), o // 16
        f_, s_ = x_ * (1 - c_) + y_ * c_, y_ * (1 - c_) + x_ * c_
        return ((c_ * 4 + s_) * 4 + f_) * 2 + z_

    def reorder(q, carry):
        two = jnp.concatenate([rb[place_of(2 * q)], rb[place_of(2 * q + 1)]], axis=0)
        high, low = split(two)
        at = pl.ds(pl.multiple_of(q * 2 * PANEL, 16), 2 * PANEL)
        rh[at] = high
        rl[at] = low
        return carry

    lax.fori_loop(0, STATES // (2 * PANEL), reorder, 0)

    result = scale * (m * (total[FIRST:] + sums_in(1)) - root_b * step)
    fg[band] = result

    b_next, b_last, b_far = lax.rem(band + 1, 4), lax.rem(band + 3, 4), lax.rem(band + 2, 4)
    bs = iter(range(6))

    def rows_to(b, h, peer):
        part = fg.at[b, pl.ds(h * HALF, HALF)]
        sends.append(send(part, part, bsend.at[next(bs)], brecv.at[b, h], peer))

    rows_to(band, 0, b_up)
    rows_to(band, 1, b_down)
    rows_to(band, 1, b_up)
    rows_to(band, 0, b_down)

    def times(values, b):
        high, low = split(values)
        at = pl.ds(pl.multiple_of(b * COLS, 128), COLS)
        return mm3(high, low, rh[at], rl[at])

    def got(b, h):
        arrived(fg.at[b, pl.ds(h * HALF, HALF)], brecv.at[b, h])

    ov[...] = times(result, band)
    got(b_last, 0)
    rows_to(b_last, 0, b_up)
    got(b_next, 1)
    rows_to(b_next, 1, b_down)
    top, bottom = pl.ds(0, HALF), pl.ds(HALF, HALF)
    ov[top] += times(fg[b_last, top], b_last)
    ov[bottom] += times(fg[b_next, bottom], b_next)
    got(b_last, 1)
    ov[bottom] += times(fg[b_last, bottom], b_last)
    got(b_next, 0)
    ov[top] += times(fg[b_next, top], b_next)
    got(b_far, 0)
    ov[top] += times(fg[b_far, top], b_far)
    got(b_far, 1)
    ov[bottom] += times(fg[b_far, bottom], b_far)

    store = pltpu.make_async_copy(ov, out, ld.at[0])
    store.start()
    for copy in sends:
        copy.wait_send()
    store.wait()


def shards(states, inv_mass, cell_ham, cell_nodes, send_up, send_down, owner, rotation_store):
    dma = pltpu.SemaphoreType.DMA
    vmem = pltpu.VMEM
    return pl.pallas_call(
        kernel,
        out_shape=jax.ShapeDtypeStruct((OWN, COLS), f32),
        in_specs=[pl.BlockSpec(memory_space=pl.ANY)] * 8,
        out_specs=pl.BlockSpec(memory_space=pl.ANY),
        scratch_shapes=[
            vmem((OWN, COLS), f32),
            vmem((1, OWN), f32),
            vmem((CELLS, CN, CN), f32),
            vmem((CELLS, CN), jnp.int32),
            vmem((1, GHOST), jnp.int32),
            vmem((1, GHOST), jnp.int32),
            pltpu.SMEM((64,), jnp.int32),
            vmem((64, PANEL, COLS), f32),
            vmem((2, 2 * GHOST, COLS), f32),
            vmem((2, 2 * GHOST, COLS), f32),
            vmem((2, 2 * GHOST, COLS), f32),
            vmem((2, 2 * GHOST, COLS), f32),
            vmem((EXT, EXT), f32),
            vmem((EXT, EXT), bf16),
            vmem((EXT, EXT), bf16),
            vmem((4, OWN, COLS), f32),
            vmem((STATES, COLS), bf16),
            vmem((STATES, COLS), bf16),
            vmem((OWN, COLS), f32),
            dma((8,)),
            dma((64,)),
            dma((4, 2)),
            dma((4, 4)),
            dma((4, 2)),
            dma((4,)),
            dma((2, 4)),
            dma((2, 4)),
            dma((6,)),
            dma((4, 2)),
        ],
        compiler_params=pltpu.CompilerParams(
            collective_id=0, has_side_effects=True, vmem_limit_bytes=56 * 1024 * 1024
        ),
    )(
        states,
        inv_mass.reshape(1, OWN),
        cell_ham,
        cell_nodes,
        send_up.reshape(1, GHOST),
        send_down.reshape(1, GHOST),
        owner,
        rotation_store,
    )


def solution(mesh):
    in_specs = (
        P("dom", "band"),
        P("dom"),
        P("dom", None, None),
        P("dom", None),
        P("dom"),
        P("dom"),
        P(),
        P("dom", None),
    )
    return jax.shard_map(
        shards, mesh=mesh, in_specs=in_specs, out_specs=P("dom", "band"), check_vma=False
    )
```

time: 193 us -> 58 us (0.30)
  Pallas kernels: 0 us -> 56.1 us
  waiting for transfers between devices: 51.5 us -> 0 us
  other arithmetic: 39.2 us -> 0 us
  local copies, waits for them, and re-layouts: 40.7 us -> 1.69 us
  starting transfers between devices: 24.5 us -> 0 us
  matrix products: 22.9 us -> 0 us
  between operations: 13.7 us -> 0.01 us
    pallas_call x0 -> x1, Pallas kernels: none -> 56.1 us  [shards(): pl.pallas_call(kernel, out_shape=jax.ShapeDtypeStruct((OWN, COLS), f32),...]
    reduce_scatter x1 -> x0, waiting for transfers between devices: 43 us -> none  [shards(): lax.psum_scatter(partial_term, 'band', scatter_dimension=1, tiled=True)]
    scatter-add x6 -> x0, other arithmetic: 31.4 us -> none  [the longest x2 26.5 us: apply_operator(): empty.at[cell_nodes.reshape(-1)].add(products.reshape(-1, block_cols))]
    gather x9 -> x0, local copies, waits for them, and re-layouts: 28.6 us -> none  [the longest x4 18 us: apply_operator(): gathered = extended[cell_nodes]]
    ppermute x8 -> x0, starting transfers between devices: 24.5 us -> none  [the longest x4 24.4 us: with_halo(): lax.ppermute(lax.slice_in_dim(block, 0, width, axis=dim), axis, backward)]
    dot_general x3 -> x0, matrix products: 22.9 us -> none  [the longest x2 18 us: apply_operator(): jnp.einsum('cij,cjs->cis', cell_ham, gathered, precision=lax.Precision.HI...]
    reshape x3 -> x0, local copies, waits for them, and re-layouts: 7.96 us -> none  [the longest x2 7.17 us: apply_operator(): products.reshape(-1, block_cols)]
    ppermute x8 -> x0, waiting for transfers between devices: 7.73 us -> none  [the longest x4 6.89 us: with_halo(): lax.ppermute(lax.slice_in_dim(block, block.shape[dim] - width, None, axis...]
  transfers between devices with their start and end apart: 10 -> 0, of which waited for: 4 -> 0; matrix products, arithmetic and copies ran while one was open for 46% -> 0% of each run, Pallas kernels for 0% -> 0%
where the time goes in v1:
time: 58 us; the launch traced here: 57.8 us
  Pallas kernels  56.1 us (97%)
  local copies, waits for them, and re-layouts  1.69 us (3%)
    pallas_call x1, Pallas kernels, shards(): pl.pallas_call(kernel, out_shape=jax.ShapeDtypeStruct((OWN, COLS), f32),...  56.1 us
    unnamed x1, local copies, waits for them, and re-layouts  1.69 us

profile of v1, /device:TPU:1, one launch (start us, length us, event | category | flops | bytes accessed | tf_op | source)
XLA Modules:
  0.0 57.8 jit_solution(1351100800122825665)
XLA Ops:
  0.0 56.1 %shard_map.82 = f32[192,384]{1,0:T(8,128)} custom-call(f32[192,384]{1,0:T(8,128)} %states.1, f32[1,192]{1,0:T(1,128)} %bitcast.3, f32[5,343,343]{2,1,0:T(8,128)} %ham.1, s32[5,343]{1,0:T(8,128)} %nodes.1, s32[1,48]{1,0:T(1,128)} %bitcast.4, s32[1,48]{1,0:T(1,128)} %bitcast.5, s32[64]{0:T(128)} %owner.1, f32[24,1536]{1,0:T(8,128)} %rot.1), custom_call_target="tpu_custom_call" | custom-call | tf_op jit(solution)/shard_map/pallas_call | solution.py:355
  56.1 1.7 %copy.10 = f32[192,384]{1,0:T(8,128)} copy(f32[192,384]{1,0:T(8,128)} %shard_map.82) | data formatting | bytes 589824

commit v2 on v1

v2 whole, which is shorter than its diff:
```python
import math

import jax
import jax.numpy as jnp
from jax import lax
from jax.experimental import pallas as pl
from jax.experimental.pallas import tpu as pltpu
from jax.sharding import PartitionSpec as P

filter_center = 2.5
filter_half = 3.5
spectrum_floor = -4.0
sigma_one = filter_half / (spectrum_floor - filter_center)
sigma_two = 1.0 / (2.0 / sigma_one - sigma_one)
scale = 2.0 * sigma_one * sigma_two / filter_half**2
root_a = filter_center + filter_half / math.sqrt(2.0)
root_b = filter_center - filter_half / math.sqrt(2.0)

OWN = 192
GHOST = 48
COLS = 384
CELLS = 5
CN = 343
EXT = 320
FIRST = 128
PANEL = 24
STATES = 1536
HALF = OWN // 2
EARLY = 128
LATE = COLS - EARLY

f32 = jnp.float32
bf16 = jnp.bfloat16


def split(x):
    high = x.astype(bf16)
    low = (x - high.astype(f32)).astype(bf16)
    return high, low


def dot(a, b):
    return jnp.dot(a, b, preferred_element_type=f32)


def mm2(pick, x):
    high, low = split(x)
    return dot(pick, high) + dot(pick, low)


def mm3(ah, al, bh, bl):
    return dot(ah, bh) + (dot(al, bh) + dot(ah, bl))


def column(row, count):
    wide = jnp.broadcast_to(row, (count, count))
    same = lax.broadcasted_iota(jnp.int32, (count, count), 0) == lax.broadcasted_iota(
        jnp.int32, (count, count), 1
    )
    return jnp.sum(jnp.where(same, wide, 0.0), axis=1, keepdims=True)


def one_hot(condition):
    return jnp.where(condition, 1.0, 0.0).astype(bf16)


def kernel(
    states, mass, ham, nodes, sup, sdn, owner, rot, out,
    xv, mv, hv, nv, upv, dnv, ownv, rb,
    gs0, gr0, rs0, rr0, gs1, gr1, rs1, rr1, gs2, gr2, rs2, rr2,
    amat, ah, al, fe, fl, rh, rl, ov,
    ld, psend, first_sem, second_sem, mate_sem,
    gsend, grecv, bsend, erecv, lrecv,
):
    d = lax.axis_index("dom")
    band = lax.axis_index("band")
    core = lax.rem(d, 2)
    y = lax.rem(d // 2, 4)
    zl = lax.rem(d // 8, 2)
    x = d // 16
    other = 1 - zl

    def dom_of(x_, y_, zl_, core_):
        return ((x_ * 2 + zl_) * 4 + y_) * 2 + core_

    def along_first(k, z):
        return dom_of(lax.rem(x + k * (1 - core), 4), lax.rem(y + k * core, 4), z, core), band

    def along_second(k):
        return dom_of(lax.rem(x + k * core, 4), lax.rem(y + k * (1 - core), 4), zl, core), band

    f0 = x * (1 - core) + y * core
    s0 = y * (1 - core) + x * core

    def slot(c, s, f, z):
        return ((c * 4 + s) * 4 + f) * 2 + z

    up = (lax.rem(d + 1, 64), band)
    down = (lax.rem(d + 63, 64), band)
    mate = (dom_of(x, y, zl, 1 - core), band)
    b_up, b_down = (d, lax.rem(band + 1, 4)), (d, lax.rem(band + 3, 4))
    firsts = [along_first(k, zl) for k in (1, 3, 2)] + [along_first(k, other) for k in (0, 1, 3, 2)]
    seconds = [along_second(k) for k in (1, 3, 2)]

    barrier = pltpu.get_barrier_semaphore()
    peers = [up, down, mate, b_up, b_down] + firsts + seconds
    for peer in peers:
        pl.semaphore_signal(barrier, inc=1, device_id=peer, device_id_type=pl.DeviceIdType.MESH)

    sends = []

    def send(src, dst, ssem, rsem, peer):
        copy = pltpu.make_async_remote_copy(
            src_ref=src, dst_ref=dst, send_sem=ssem, recv_sem=rsem,
            device_id=peer, device_id_type=pl.DeviceIdType.MESH,
        )
        copy.start()
        sends.append(copy)

    def arrived(dst, rsem):
        pltpu.make_async_copy(dst, dst, rsem).wait()

    my_columns = rot.at[:, pl.ds(pl.multiple_of(band * COLS, 128), COLS)]
    loads = [
        pltpu.make_async_copy(states, xv, ld.at[0]),
        pltpu.make_async_copy(mass, mv, ld.at[1]),
        pltpu.make_async_copy(sup, upv, ld.at[2]),
        pltpu.make_async_copy(sdn, dnv, ld.at[3]),
        pltpu.make_async_copy(nodes, nv, ld.at[4]),
        pltpu.make_async_copy(ham, hv, ld.at[5]),
        pltpu.make_async_copy(my_columns, rb.at[slot(core, s0, f0, zl)], ld.at[6]),
        pltpu.make_async_copy(owner, ownv, ld.at[7]),
    ]
    for load in loads:
        load.start()

    for load in loads[:4]:
        load.wait()
    up_row, down_row = upv[...], dnv[...]
    m = column(mv[...], OWN)
    lanes = lax.broadcasted_iota(jnp.int32, (GHOST, OWN), 1)
    pick_up = one_hot(column(up_row.astype(f32), GHOST).astype(jnp.int32) == lanes)
    pick_down = one_hot(column(down_row.astype(f32), GHOST).astype(jnp.int32) == lanes)
    rows = lax.broadcasted_iota(jnp.int32, (OWN, GHOST), 0)
    add_up = one_hot(rows == up_row)
    add_down = one_hot(rows == down_row)
    states_scaled = xv[...] * m
    low_part, high_part = pl.ds(0, GHOST), pl.ds(GHOST, GHOST)
    ghost_send, ghost_recv = (gs0, gs1, gs2), (gr0, gr1, gr2)
    sum_send, sum_recv = (rs0, rs1, rs2), (rr0, rr1, rr2)

    def ghosts_out(k, values):
        src, dst = ghost_send[k], ghost_recv[k]
        high, low = split(values)
        src[low_part] = dot(pick_up, high) + dot(pick_up, low)
        send(src.at[low_part], dst.at[low_part], gsend.at[k, 0], grecv.at[k, 0], up)
        src[high_part] = dot(pick_down, high) + dot(pick_down, low)
        send(src.at[high_part], dst.at[high_part], gsend.at[k, 1], grecv.at[k, 1], down)

    def apply_own(values):
        high, low = split(values)
        return mm3(ah[:, FIRST:], al[:, FIRST:], high, low)

    def ghosts_in(k):
        arrived(ghost_recv[k].at[low_part], grecv.at[k, 0])
        arrived(ghost_recv[k].at[high_part], grecv.at[k, 1])
        high, low = split(ghost_recv[k][...])
        return mm3(ah[:, : 2 * GHOST], al[:, : 2 * GHOST], high, low)

    def sums_out(k, total):
        src, dst = sum_send[k], sum_recv[k]
        src[...] = total[: 2 * GHOST]
        send(src.at[low_part], dst.at[low_part], gsend.at[k, 2], grecv.at[k, 2], down)
        send(src.at[high_part], dst.at[high_part], gsend.at[k, 3], grecv.at[k, 3], up)

    def sums_in(k):
        arrived(sum_recv[k].at[low_part], grecv.at[k, 2])
        arrived(sum_recv[k].at[high_part], grecv.at[k, 3])
        return mm2(add_up, sum_recv[k][low_part]) + mm2(add_down, sum_recv[k][high_part])

    def one_cell(c):
        node = nv[pl.ds(c, 1)]
        where = jnp.where(node < OWN, node + FIRST, node - OWN)
        place = one_hot(lax.broadcasted_iota(jnp.int32, (EXT, CN), 0) == where)
        high, low = split(hv[c])
        nt = (((1,), (1,)), ((), ()))
        half = lax.dot_general(high, place, nt, preferred_element_type=f32)
        half = half + lax.dot_general(low, place, nt, preferred_element_type=f32)
        total = mm2(place, half)
        if c == 0:
            amat[...] = total
        else:
            amat[...] += total

    pl.semaphore_wait(barrier, len(peers))

    ghosts_out(0, states_scaled)

    number = iter(range(32))
    for peer in firsts:
        send(my_columns, rb.at[slot(core, s0, f0, zl)], psend.at[next(number)], first_sem.at[f0, zl], peer)

    def four(c, s, h):
        return rb.at[pl.ds(slot(c, s, 2 * h, 0), 4)]

    def spread(h):
        for peer in seconds:
            send(four(core, s0, h), four(core, s0, h), psend.at[next(number)], second_sem.at[s0, h], peer)

    def pass_on(s, h):
        send(four(core, s, h), four(core, s, h), psend.at[next(number)], mate_sem.at[s, h], mate)

    loads[4].wait()
    loads[5].wait()
    for c in range(CELLS):
        one_cell(c)
    ahv, alv = split(amat[...])
    ah[...] = ahv
    al[...] = alv
    total = apply_own(states_scaled)
    total = total + ghosts_in(0)
    sums_out(0, total)

    for k in (1, 3, 2):
        f = lax.rem(f0 + k, 4)
        arrived(rb.at[slot(core, s0, f, zl)], first_sem.at[f, zl])
    for k in (0, 1, 3, 2):
        f = lax.rem(f0 + k, 4)
        arrived(rb.at[slot(core, s0, f, other)], first_sem.at[f, other])
    loads[6].wait()
    spread(0)
    pass_on(s0, 0)
    pass_on(s0, 1)

    b_next, b_last, b_far = lax.rem(band + 1, 4), lax.rem(band + 3, 4), lax.rem(band + 2, 4)
    bnumber = iter(range(12))
    top, bottom = pl.ds(0, HALF), pl.ds(HALF, HALF)
    halves = (top, bottom)

    def rows_to(buf, recv, b, h, peer):
        part = buf.at[b, halves[h]]
        send(part, part, bsend.at[next(bnumber)], recv.at[b, h], peer)

    def over_band(buf, recv):
        rows_to(buf, recv, band, 0, b_up)
        rows_to(buf, recv, band, 1, b_down)
        rows_to(buf, recv, band, 1, b_up)
        rows_to(buf, recv, band, 0, b_down)

    def got(buf, recv, b, h):
        arrived(buf.at[b, halves[h]], recv.at[b, h])

    def relay(buf, recv):
        got(buf, recv, b_last, 0)
        rows_to(buf, recv, b_last, 0, b_up)
        got(buf, recv, b_next, 1)
        rows_to(buf, recv, b_next, 1, b_down)

    step = m * (total[FIRST:] + sums_in(0)) - root_a * xv[...]
    fe[band] = step[:, :EARLY]
    over_band(fe, erecv)
    late = step[:, EARLY:]
    late_scaled = late * m
    ghosts_out(1, late_scaled)
    spread(1)
    total = apply_own(late_scaled)
    relay(fe, erecv)
    total = total + ghosts_in(1)
    sums_out(1, total)

    for h in range(2):
        for k in (1, 3, 2):
            s = lax.rem(s0 + k, 4)
            arrived(four(core, s, h), second_sem.at[s, h])
            pass_on(s, h)

    late = scale * (m * (total[FIRST:] + sums_in(1)) - root_b * late)
    fl[band] = late
    over_band(fl, lrecv)

    for k in (0, 1, 3, 2):
        s = lax.rem(f0 + k, 4)
        for h in range(2):
            arrived(four(1 - core, s, h), mate_sem.at[s, h])
    loads[7].wait()

    def place_of(p):
        o = ownv[p]
        c_, y_, z_, x_ = lax.rem(o, 2), lax.rem(o // 2, 4), lax.rem(o // 8, 2), o // 16
        f_, s_ = x_ * (1 - c_) + y_ * c_, y_ * (1 - c_) + x_ * c_
        return slot(c_, s_, f_, z_)

    def reorder(q, carry):
        two = jnp.concatenate([rb[place_of(2 * q)], rb[place_of(2 * q + 1)]], axis=0)
        high, low = split(two)
        at = pl.ds(pl.multiple_of(q * 2 * PANEL, 16), 2 * PANEL)
        rh[at] = high
        rl[at] = low
        return carry

    lax.fori_loop(0, STATES // (2 * PANEL), reorder, 0)

    def times(values, b, first, count):
        high, low = split(values)
        at = pl.ds(pl.multiple_of(b * COLS + first, 128), count)
        return mm3(high, low, rh[at], rl[at])

    got(fe, erecv, b_last, 1)
    got(fe, erecv, b_next, 0)
    got(fe, erecv, b_far, 0)
    got(fe, erecv, b_far, 1)
    turned = times(fe[0], 0, 0, EARLY) + times(fe[1], 1, 0, EARLY)
    turned = turned + (times(fe[2], 2, 0, EARLY) + times(fe[3], 3, 0, EARLY))
    turned_scaled = turned * m
    ghosts_out(2, turned_scaled)
    total = apply_own(turned_scaled)
    relay(fl, lrecv)
    ov[...] = times(late, band, EARLY, LATE)
    ov[top] += times(fl[b_last, top], b_last, EARLY, LATE)
    ov[bottom] += times(fl[b_next, bottom], b_next, EARLY, LATE)
    total = total + ghosts_in(2)
    sums_out(2, total)
    got(fl, lrecv, b_last, 1)
    ov[bottom] += times(fl[b_last, bottom], b_last, EARLY, LATE)
    got(fl, lrecv, b_next, 0)
    ov[top] += times(fl[b_next, top], b_next, EARLY, LATE)
    ov[...] += scale * (m * (total[FIRST:] + sums_in(2)) - root_b * turned)
    got(fl, lrecv, b_far, 0)
    ov[top] += times(fl[b_far, top], b_far, EARLY, LATE)
    got(fl, lrecv, b_far, 1)
    ov[bottom] += times(fl[b_far, bottom], b_far, EARLY, LATE)

    store = pltpu.make_async_copy(ov, out, ld.at[0])
    store.start()
    for copy in sends:
        copy.wait_send()
    store.wait()


def shards(states, inv_mass, cell_ham, cell_nodes, send_up, send_down, owner, rotation_store):
    dma = pltpu.SemaphoreType.DMA
    vmem = pltpu.VMEM
    edges = [vmem((2 * GHOST, n), f32) for n in (COLS, LATE, COLS) for _ in range(4)]
    return pl.pallas_call(
        kernel,
        out_shape=jax.ShapeDtypeStruct((OWN, COLS), f32),
        in_specs=[pl.BlockSpec(memory_space=pl.ANY)] * 8,
        out_specs=pl.BlockSpec(memory_space=pl.ANY),
        scratch_shapes=[
            vmem((OWN, COLS), f32),
            vmem((1, OWN), f32),
            vmem((CELLS, CN, CN), f32),
            vmem((CELLS, CN), jnp.int32),
            vmem((1, GHOST), jnp.int32),
            vmem((1, GHOST), jnp.int32),
            pltpu.SMEM((64,), jnp.int32),
            vmem((64, PANEL, COLS), f32),
            *edges,
            vmem((EXT, EXT), f32),
            vmem((EXT, EXT), bf16),
            vmem((EXT, EXT), bf16),
            vmem((4, OWN, EARLY), f32),
            vmem((4, OWN, LATE), f32),
            vmem((STATES, COLS), bf16),
            vmem((STATES, COLS), bf16),
            vmem((OWN, COLS), f32),
            dma((8,)),
            dma((32,)),
            dma((4, 2)),
            dma((4, 2)),
            dma((4, 2)),
            dma((3, 4)),
            dma((3, 4)),
            dma((12,)),
            dma((4, 2)),
            dma((4, 2)),
        ],
        compiler_params=pltpu.CompilerParams(
            collective_id=0, has_side_effects=True, vmem_limit_bytes=56 * 1024 * 1024
        ),
    )(
        states,
        inv_mass.reshape(1, OWN),
        cell_ham,
        cell_nodes,
        send_up.reshape(1, GHOST),
        send_down.reshape(1, GHOST),
        owner,
        rotation_store,
    )


def solution(mesh):
    in_specs = (
        P("dom", "band"),
        P("dom"),
        P("dom", None, None),
        P("dom", None),
        P("dom"),
        P("dom"),
        P(),
        P("dom", None),
    )
    return jax.shard_map(
        shards, mesh=mesh, in_specs=in_specs, out_specs=P("dom", "band"), check_vma=False
    )
```

time: 58 us -> 52.3 us (0.902)
  Pallas kernels: 56.1 us -> 50.4 us
    pallas_call x1, Pallas kernels: 56.1 us -> 50.4 us  [shards(): pl.pallas_call(kernel, out_shape=jax.ShapeDtypeStruct((OWN, COLS), f32),...]
where the time goes in v2:
time: 52.3 us; the launch traced here: 52.1 us
  Pallas kernels  50.4 us (96%)
  local copies, waits for them, and re-layouts  1.69 us (3%)
    pallas_call x1, Pallas kernels, shards(): pl.pallas_call(kernel, out_shape=jax.ShapeDtypeStruct((OWN, COLS), f32),...  50.4 us
    unnamed x1, local copies, waits for them, and re-layouts  1.69 us

profile of v2, /device:TPU:1, one launch (start us, length us, event | category | flops | bytes accessed | tf_op | source)
XLA Modules:
  0.0 52.1 jit_solution(6729972707885049565)
XLA Ops:
  0.0 50.4 %shard_map.82 = f32[192,384]{1,0:T(8,128)} custom-call(f32[192,384]{1,0:T(8,128)} %states.1, f32[1,192]{1,0:T(1,128)} %bitcast.3, f32[5,343,343]{2,1,0:T(8,128)} %ham.1, s32[5,343]{1,0:T(8,128)} %nodes.1, s32[1,48]{1,0:T(1,128)} %bitcast.4, s32[1,48]{1,0:T(1,128)} %bitcast.5, s32[64]{0:T(128)} %owner.1, f32[24,1536]{1,0:T(8,128)} %rot.1), custom_call_target="tpu_custom_call" | custom-call | tf_op jit(solution)/shard_map/pallas_call | solution.py:344
  50.4 1.7 %copy.10 = f32[192,384]{1,0:T(8,128)} copy(f32[192,384]{1,0:T(8,128)} %shard_map.82) | data formatting | bytes 589824

commit v3 on v2

--- a/solution.py
+++ b/solution.py
@@ -65,10 +65,10 @@
 
 
 def kernel(
-    states, mass, ham, nodes, sup, sdn, owner, rot, out,
+    states, mass, ham, nodes, sup, sdn, owner, rot, ov,
     xv, mv, hv, nv, upv, dnv, ownv, rb,
     gs0, gr0, rs0, rr0, gs1, gr1, rs1, rr1, gs2, gr2, rs2, rr2,
-    amat, ah, al, fe, fl, rh, rl, ov,
+    amat, ah, al, fe, fl, rh, rl,
     ld, psend, first_sem, second_sem, mate_sem,
     gsend, grecv, bsend, erecv, lrecv,
 ):
@@ -330,11 +330,8 @@
     got(fl, lrecv, b_far, 1)
     ov[bottom] += times(fl[b_far, bottom], b_far, EARLY, LATE)
 
-    store = pltpu.make_async_copy(ov, out, ld.at[0])
-    store.start()
     for copy in sends:
         copy.wait_send()
-    store.wait()
 
 
 def shards(states, inv_mass, cell_ham, cell_nodes, send_up, send_down, owner, rotation_store):
@@ -343,9 +340,9 @@
     edges = [vmem((2 * GHOST, n), f32) for n in (COLS, LATE, COLS) for _ in range(4)]
     return pl.pallas_call(
         kernel,
-        out_shape=jax.ShapeDtypeStruct((OWN, COLS), f32),
+        out_shape=vmem((OWN, COLS), f32),
         in_specs=[pl.BlockSpec(memory_space=pl.ANY)] * 8,
-        out_specs=pl.BlockSpec(memory_space=pl.ANY),
+        out_specs=pl.BlockSpec(memory_space=pltpu.VMEM),
         scratch_shapes=[
             vmem((OWN, COLS), f32),
             vmem((1, OWN), f32),
@@ -363,7 +360,6 @@
             vmem((4, OWN, LATE), f32),
             vmem((STATES, COLS), bf16),
             vmem((STATES, COLS), bf16),
-            vmem((OWN, COLS), f32),
             dma((8,)),
             dma((32,)),
             dma((4, 2)),

time: 52.3 us -> 50.6 us (0.967)
  local copies, waits for them, and re-layouts: 1.69 us -> 0.72 us
  Pallas kernels: 50.4 us -> 49.8 us
    unnamed x1, local copies, waits for them, and re-layouts: 1.69 us -> 0.72 us
    pallas_call x1, Pallas kernels: 50.4 us -> 49.8 us  [shards(): pl.pallas_call(kernel, out_shape=vmem((OWN, COLS), f32), in_specs=[pl.Blo...]
where the time goes in v3:
time: 50.6 us; the launch traced here: 50.5 us
  Pallas kernels  49.8 us (98%)
  local copies, waits for them, and re-layouts  0.72 us (1%)
    pallas_call x1, Pallas kernels, shards(): pl.pallas_call(kernel, out_shape=vmem((OWN, COLS), f32), in_specs=[pl.Blo...  49.8 us

profile of v3, /device:TPU:1, one launch (start us, length us, event | category | flops | bytes accessed | tf_op | source)
XLA Modules:
  0.0 50.5 jit_solution(16003635252620459748)
XLA Ops:
  0.0 49.8 %shard_map.82 = f32[192,384]{1,0:T(8,128)S(1)} custom-call(f32[192,384]{1,0:T(8,128)} %states.1, f32[1,192]{1,0:T(1,128)} %bitcast.3, f32[5,343,343]{2,1,0:T(8,128)} %ham.1, s32[5,343]{1,0:T(8,128)} %nodes.1, s32[1,48]{1,0:T(1,128)} %bitcast.4, s32[1,48]{1,0:T(1,128)} %bitcast.5, s32[64]{0:T(128)} %owner.1, f32[24,1536]{1,0:T(8,128)} %rot.1), custom_call_target="tpu_custom_call" | custom-call | tf_op jit(solution)/shard_map/pallas_call | solution.py:341
  49.8 0.7 %copy.10 = f32[192,384]{1,0:T(8,128)} copy(f32[192,384]{1,0:T(8,128)S(1)} %shard_map.82) | data formatting | bytes 589824
